TPU v7x, 32 devices: a whole 2x2x4 slice. The times are simulated.
32 devices in a mesh: row: 8 (over z, y), col: 4 (over x, core).
Axes of the slice: x: 2, y: 2, z: 4, core: 2. Of those that a mesh axis runs over, the one named last changes fastest.
Arguments:
- inv_interior: bfloat16 [64, 1024, 1024], P(('row', 'col')), may hold values from -1 to 3
- coupling: bfloat16 [64, 1024, 512], P(('row', 'col')), may hold values from -0.375 to 0.375
- boundary_stiff: bfloat16 [64, 512, 512], P(('row', 'col')), may hold values from -6 to 6
- mass_interior: float32 [64, 1024], P(('row', 'col')), may hold values from 0.5 to 2
- mass_boundary: float32 [64, 512], P(('row', 'col')), may hold values from 0.5 to 2
- block_map: int32 [64, 4], P(('row', 'col')), may hold values from 0 to 127, as said below
- modes: bfloat16 [16384, 1024], P('col', 'row'), may hold values from -0.046875 to 0.046875
Outputs:
- iface_stiff: bfloat16 [16384, 16384], P('row', 'col')
- iface_mass: bfloat16 [16384, 16384], P('row', 'col')
- reduced_stiff: float32 [1024, 1024], P(('row', 'col'))
- reduced_mass: float32 [1024, 1024], P(('row', 'col'))
- mass_diagonal: float32 [16384], P(('row', 'col'))
Inputs may be any that keep to these rules, and one draw needn't show every extreme that they name: Interface block p belongs to tile row p // 16 and tile column p // 32; the pair (block_map[s, a], block_map[s, b]) belongs to the tile of its row's tile row and its column's tile column. Over the 2 substructures of one device (aligned blocks of rows), no two triples (s, a, b) fall into the same tile, and in every draw some tile receives a pair from every device.
All inputs are finite; a program needn't handle non-finite values.
Results may differ from a plain program's by a relative error of at most 0.0058.
Values may be sent and summed in bfloat16 or wider, within the bound.
No kernel may reach another device: no remote copies, remote signals or barrier semaphores. Data moves between devices by JAX's collectives and lax.ppermute only.
A program may use at most 192 MiB of HBM per device.

v0:
```python
import jax
import jax.numpy as jnp
from jax import lax
from jax.sharding import PartitionSpec as P

BLK = 128


def broadcast(value, axis, source):
    kept = jnp.where(lax.axis_index(axis) == source, value, 0).astype(value.dtype)
    return lax.psum(kept, axis)


def condense(pieces):
    inverse, couple, stiffness, interior_mass, boundary_mass = pieces
    static_modes = (-jnp.dot(inverse, couple, preferred_element_type=jnp.float32)).astype(
        jnp.bfloat16
    )
    stiff_cond = stiffness.astype(jnp.float32) + jnp.dot(
        couple.T, static_modes, preferred_element_type=jnp.float32
    )
    weighted = (static_modes.astype(jnp.float32) * interior_mass[:, None]).astype(jnp.bfloat16)
    mass_cond = jnp.dot(static_modes.T, weighted, preferred_element_type=jnp.float32) + jnp.diag(
        boundary_mass
    )
    return jnp.stack([stiff_cond, mass_cond])


def body(inv_interior, coupling, boundary_stiff, mass_interior, mass_boundary, block_map, modes):
    row_count = lax.axis_size("row")
    col_count = lax.axis_size("col")
    device_count = row_count * col_count
    local_subs, interior_width, boundary_width = coupling.shape
    per_sub = boundary_width // BLK
    tile_cols = modes.shape[0]
    tile_rows = tile_cols * col_count // row_count
    mode_count = modes.shape[1] * row_count
    row_blocks = tile_rows // BLK
    col_blocks = tile_cols // BLK
    row_index = lax.axis_index("row")
    col_index = lax.axis_index("col")
    ratio_rows = row_count // col_count
    share_rows = tile_rows // col_count
    condensed = lax.map(
        condense, (inv_interior, coupling, boundary_stiff, mass_interior, mass_boundary)
    )
    blocks = condensed.reshape(local_subs, 2, per_sub, BLK, per_sub, BLK).transpose(
        0, 2, 4, 1, 3, 5
    )
    blocks = blocks.reshape(local_subs * per_sub * per_sub, 2, BLK, BLK)
    block_rows = jnp.broadcast_to(block_map[:, :, None], (local_subs, per_sub, per_sub)).reshape(-1)
    block_cols = jnp.broadcast_to(block_map[:, None, :], (local_subs, per_sub, per_sub)).reshape(-1)
    owner_index = block_rows // row_blocks * col_count + block_cols // col_blocks
    slot_index = block_rows % row_blocks * col_blocks + block_cols % col_blocks
    matches = owner_index[None, :] == jnp.arange(device_count, dtype=jnp.int32)[:, None]
    filled = jnp.any(matches, axis=1)
    chosen = jnp.argmax(matches, axis=1)
    outgoing = jnp.take(blocks, chosen, axis=0) * filled[:, None, None, None].astype(jnp.float32)
    targets = jnp.where(filled, jnp.take(slot_index, chosen), -1)
    arrived, arrived_slots = (
        lax.all_to_all(outgoing, ("row", "col"), split_axis=0, concat_axis=0, tiled=True),
        lax.all_to_all(targets, ("row", "col"), split_axis=0, concat_axis=0, tiled=True),
    )
    summed_blocks = jax.ops.segment_sum(
        arrived, jnp.maximum(arrived_slots, 0), num_segments=row_blocks * col_blocks
    )
    full_pair = summed_blocks.reshape(row_blocks, col_blocks, 2, BLK, BLK).transpose(2, 0, 3, 1, 4)
    full_pair = full_pair.reshape(2, tile_rows, tile_cols)
    holder = col_index == row_index // ratio_rows
    offset = row_index % ratio_rows * tile_rows
    column_ids = jnp.arange(tile_cols, dtype=jnp.int32)[None, :]
    row_ids = jnp.arange(tile_rows, dtype=jnp.int32)[:, None]
    on_diagonal = jnp.logical_and(column_ids == row_ids + offset, holder)
    mass_tile = full_pair[1]
    diag_local = jnp.sum(jnp.where(on_diagonal, mass_tile, jnp.float32(0.0)), axis=1)
    mass_share = lax.psum_scatter(diag_local, "col", scatter_dimension=0, tiled=True)
    stiff_tile = full_pair[0].astype(jnp.bfloat16)
    mass_off = jnp.where(on_diagonal, jnp.float32(0.0), mass_tile).astype(jnp.bfloat16)
    col_modes = lax.all_gather(modes, "row", axis=1, tiled=True)
    mode_slab = lax.dynamic_slice_in_dim(
        col_modes, row_index % ratio_rows * tile_rows, tile_rows, 0
    )
    row_modes = broadcast(mode_slab, "col", row_index // ratio_rows)
    right_side = jnp.concatenate(
        [
            jnp.dot(stiff_tile, col_modes, preferred_element_type=jnp.float32),
            jnp.dot(mass_off, col_modes, preferred_element_type=jnp.float32),
        ],
        1,
    )
    left_modes = row_modes.astype(jnp.float32)
    share_start = col_index * share_rows
    share_modes = lax.dynamic_slice_in_dim(left_modes, share_start, share_rows, 0)
    mass_part = lax.dynamic_slice(
        right_side, (share_start, jnp.int32(mode_count)), (share_rows, mode_count)
    )
    right_side = lax.dynamic_update_slice(
        right_side,
        mass_part + mass_share[:, None] * share_modes,
        (share_start, jnp.int32(mode_count)),
    )
    reduced = lax.psum_scatter(
        jnp.dot(
            left_modes.T,
            right_side,
            precision=lax.Precision.HIGHEST,
            preferred_element_type=jnp.float32,
        ),
        ("row", "col"),
        scatter_dimension=0,
        tiled=True,
    )
    return (stiff_tile, mass_off, reduced[:, :mode_count], reduced[:, mode_count:], mass_share)


def solution(mesh):
    return jax.shard_map(
        body,
        mesh=mesh,
        in_specs=(
            P(("row", "col"), None, None),
            P(("row", "col"), None, None),
            P(("row", "col"), None, None),
            P(("row", "col"), None),
            P(("row", "col"), None),
            P(("row", "col"), None),
            P("col", "row"),
        ),
        out_specs=(
            P("row", "col"),
            P("row", "col"),
            P(("row", "col"), None),
            P(("row", "col"), None),
            P(("row", "col")),
        ),
        check_vma=False,
    )
```

profile of v0, /device:TPU:0, one launch (start us, length us, event | category | flops | bytes accessed | tf_op | source)
XLA Modules:
  0.0 656.3 jit_solution(4957446809778439733)
XLA Ops:
  11.0 7.3 %all-to-all-start = ((s32[32,1,1]{2,1,0:T(1,128)}), s32[32,1,1]{2,1,0:T(1,128)S(1)}, u32[]{:S(2)}, u32[]{:S(2)}) async-start(s32[32,1,1]{2,1,0:T(1,128)} %copy.28), calls=%async_computation | async-start | bytes 32768 | tf_op jit(solution)/shard_map/all_to_all | solution.py:62
  18.3 14.7 %while.10 = (s32[]{:T(128)}, f32[2,2,512,512]{3,2,1,0:T(8,128)}, bf16[2,512,512]{2,1,0:T(8,128)(2,1)}, bf16[2,1024,512]{2,1,0:T(8,128)(2,1)}, bf16[2,1024,1024]{...) while((s32[]{:T(128)}, f32[2,2,512,512]{3,2,1,0:T(8,128)}, ...), condition=%wide.region_3.4_spmd, body=%wide.region_2.3_spmd.sunk | while | flops 2151940096 | bytes 60363024 | solution.py:44
  33.0 5.2 reshape.158
  38.2 4.8 copy.29
  43.0 5.0 gather_fusion.1
  48.0 5.2 select_multiply_fusion
  53.2 6.0 all-to-all-start.1
  62.8 171.5 %all-to-all-done.1 = f32[32,2,128,128]{3,2,1,0:T(8,128)} async-done(((f32[32,2,128,128]{3,2,1,0:T(8,128)}), f32[32,2,128,128]{3,2,1,0:T(8,128)}, u32[]{:S(2)}, u32[]{:S(2)}) %all-to-all-start.1) | async-done | bytes 4194336 | tf_op jit(solution)/shard_map/all_to_all | solution.py:61
  234.3 21.2 %broadcast_in_dim.82 = f32[512,2,128,128]{3,2,1,0:T(8,128)} broadcast(f32[]{:T(128)} %constant.133.clone.1), dimensions={} | broadcast | bytes 67108864 | tf_op jit(solution)/shard_map/broadcast_in_dim | solution.py:64
  255.6 9.7 %scatter_fusion = f32[512,2,128,128]{3,2,1,0:T(8,128)} fusion(f32[512,2,128,128]{3,2,1,0:T(8,128)} %broadcast_in_dim.82, s32[32]{0:T(128)S(1)} %maximum_reduce_fusion, f32[32,2,128,128]{3,2,1,0:T(8,128)} %all-to-all-done.1), kind=kCustom, calls=%fused_computation.2 | custom fusion | flops 1048576 | bytes 12583040 | tf_op jit(solution)/shard_map/scatter-add | solution.py:64
  265.3 27.9 %fusion.25 = (bf16[1,16,128,32,128]{4,2,0,3,1:T(8,128)(2,1)S(1)}, bf16[1,16,128,32,128]{4,2,0,3,1:T(8,128)(2,1)}) fusion(f32[2,16,128,32,128]{4,2,0,3,1:T(8,128)} %bitcast.12), kind=kLoop, calls=%fused_computation.64 | loop fusion | bytes 67108864 | tf_op jit(solution)/shard_map/slice | solution.py:74
  293.2 14.7 %copy.30 = bf16[1,16,128,32,128]{4,3,2,1,0:T(8,128)(2,1)S(1)} copy(bf16[1,16,128,32,128]{4,2,0,3,1:T(8,128)(2,1)} %get-tuple-element.62) | data formatting | bytes 33554432 | tf_op jit(solution)/shard_map/slice | solution.py:77
  307.9 11.0 %copy.37 = bf16[256,8,32,128]{3,1,2,0:T(8,128)(2,1)} copy(bf16[256,8,32,128]{3,2,1,0:T(8,128)(2,1)S(1)} %bitcast.76) | data formatting | bytes 33554432
  318.9 11.6 %copy.31 = bf16[1,16,128,32,128]{4,3,2,1,0:T(8,128)(2,1)} copy(bf16[1,16,128,32,128]{4,2,0,3,1:T(8,128)(2,1)S(1)} %get-tuple-element.61) | data formatting | bytes 33554432 | tf_op jit(solution)/shard_map/slice | solution.py:74
  330.5 14.6 %select_reduce_fusion = f32[16,128]{1,0:T(8,128)S(1)} fusion(s32[16,128]{1,0:T(8,128)S(1)} %add_add_fusion, s32[32,128]{1,0:T(8,128)S(1)} %multiply_add_fusion, pred[]{:T(512)S(6)} %eq.67, f32[2,16,128,32,128]{4,2,0,3,1:T(8,128)} %bitcast.12), kind=kLoop, calls=%fused_computation.28 | loop fusion | flops 33552384 | bytes 33587200 | tf_op jit(solution)/shard_map/reduce_sum | solution.py:75
  345.1 5.8 all-reduce
  350.9 21.1 %fusion.17 = bf16[2048,4096]{1,0:T(8,128)(2,1)} fusion(bf16[256,8,32,128]{3,2,1,0:T(8,128)(2,1)} %bitcast.75, s32[2048]{0:T(1024)S(1)} %iota_add_fusion, pred[]{:T(512)S(6)} %eq.67), kind=kLoop, calls=%fused_computation.26 | loop fusion | flops 25165824 | bytes 33562624 | tf_op jit(solution)/shard_map/convert_element_type | solution.py:78
  372.1 5.5 dynamic-slice_select_fusion
  377.8 21.7 %fusion.28 = f32[2048,1024]{0,1:T(8,128)S(1)} fusion(bf16[2048,4096]{1,0:T(8,128)(2,1)} %fusion.17, bf16[4096,1024]{0,1:T(8,128)(2,1)} %all-gather.2.cloned.1.call-done), kind=kOutput, calls=%fused_computation.67 | convolution fusion | flops 17179869184 | bytes 33554432 | tf_op jit(solution)/shard_map/dot_general | solution.py:87
  399.5 24.7 %fusion.27 = f32[2048,1024]{0,1:T(8,128)S(1)} fusion(bf16[2048,4096]{1,0:T(8,128)(2,1)} %bitcast.77, bf16[4096,1024]{0,1:T(8,128)(2,1)} %all-gather.2.cloned.1.call-done), kind=kOutput, calls=%fused_computation.66 | convolution fusion | flops 17179869184 | bytes 33554432 | tf_op jit(solution)/shard_map/dot_general | solution.py:86
  427.5 6.3 pad_maximum_fusion
  433.9 29.6 %all-reduce.3.cloned.1.call-done = bf16[2048,1024]{0,1:T(8,128)(2,1)} async-done(((bf16[2048,1024]{0,1:T(8,128)(2,1)}), bf16[2048,1024]{0,1:T(8,128)(2,1)}) %all-reduce.3.cloned.1.call-update) | async-done | bytes 4194320 | tf_op jit(solution)/shard_map/psum | solution.py:11
  467.3 30.5 %fusion.29 = f32[1024,2048]{1,0:T(8,128)} fusion(bf16[2048,1024]{0,1:T(8,128)(2,1)S(1)} %copy-done.5, f32[2048,2048]{0,1:T(8,128)} %fusion.21), kind=kOutput, calls=%fused_computation.68 | convolution fusion | flops 51539607552 | bytes 29360128 | tf_op jit(solution)/shard_map/dot_general | solution.py:103
  497.7 150.4 %reduce-scatter.2.cloned.1.call-done = f32[32,2048]{1,0:T(8,128)} async-done(((f32[1024,2048]{1,0:T(8,128)}), f32[32,2048]{1,0:T(8,128)}) %reduce-scatter.2.cloned.1.call-update) | async-done | bytes 262160 | tf_op jit(solution)/shard_map/reduce_scatter | solution.py:102
  (79 shorter events, 30.3 us)
Async XLA Ops:
  11.0 42.2 %all-to-all-start = ((s32[32,1,1]{2,1,0:T(1,128)}), s32[32,1,1]{2,1,0:T(1,128)S(1)}, u32[]{:S(2)}, u32[]{:S(2)}) async-start(s32[32,1,1]{2,1,0:T(1,128)} %copy.28), calls=%async_computation | async-start | bytes 32768 | tf_op jit(solution)/shard_map/all_to_all | solution.py:62
  18.3 3.3 copy-start.6
  18.3 3.3 copy-start.7
  18.4 4.2 copy-start.9
  18.4 4.2 copy-start.10
  18.4 5.0 copy-start.2
  23.6 2.0 copy-start.3
  25.7 3.3 copy-start.6
  25.7 3.3 copy-start.7
  25.7 4.2 copy-start.9
  25.7 4.2 copy-start.10
  25.7 5.0 copy-start.2
  31.0 2.0 copy-start.3
  48.0 11.2 %copy-start.4 = (bf16[4096,128]{1,0:T(8,128)(2,1)S(1)}, bf16[4096,128]{1,0:T(8,128)(2,1)}, u32[]{:S(2)}) copy-start(bf16[4096,128]{1,0:T(8,128)(2,1)} %param.15) | copy-start | bytes 3145732
  48.0 12.9 %copy-start.11 = (u32[32]{0:T(128)S(1)}, u32[32]{0:T(128)}, u32[]{:S(2)}) copy-start(u32[32]{0:T(128)} %constant.164) | copy-start | bytes 388
  53.2 181.1 %all-to-all-start.1 = ((f32[32,2,128,128]{3,2,1,0:T(8,128)}), f32[32,2,128,128]{3,2,1,0:T(8,128)}, u32[]{:S(2)}, u32[]{:S(2)}) async-start(f32[32,2,128,128]{3,2,1,0:T(8,128)} %select_multiply_fusion), calls=%async_computation.1 | async-start | bytes 8388608 | tf_op jit(solution)/shard_map/all_to_all | solution.py:61
  59.2 312.9 %all-gather.2.cloned.1.call-start = ((), (), s32[]{:S(2)}) async-start(), calls=%async_computation.3 | async-start | bytes 9437184 | tf_op jit(solution)/shard_map/all_gather | solution.py:79
  60.6 402.9 %all-reduce.3.cloned.1.call-start = ((), (), s32[]{:S(2)}) async-start(), calls=%async_computation.4 | async-start | bytes 8388608 | tf_op jit(solution)/shard_map/psum | solution.py:11
  350.9 112.6 %copy-start.8 = (f32[512]{0:T(512)}, f32[512]{0:T(512)S(1)}, u32[]{:S(2)}) copy-start(f32[512]{0:T(512)S(1)} %dynamic-slice.1) | copy-start | bytes 6148
  377.5 270.6 %reduce-scatter.2.cloned.1.call-start = ((), (), s32[]{:S(2)}) async-start(), calls=%async_computation.5 | async-start | bytes 8650752 | tf_op jit(solution)/shard_map/reduce_scatter | solution.py:102
  399.5 24.7 %copy-start = (f32[2048,1024]{0,1:T(8,128)}, f32[2048,1024]{0,1:T(8,128)S(1)}, u32[]{:S(2)}) copy-start(f32[2048,1024]{0,1:T(8,128)S(1)} %fusion.28) | copy-start | bytes 25165828
  424.2 3.3 copy-start.1
  463.5 3.8 copy-start.5
Sparse Core Ops, SparseCore 0:
  62.1 192.2 all-gather.1
  377.6 85.7 all-reduce.2
  497.9 150.1 reduce-scatter.1
where the time goes:
time: 657 us; the launch traced here: 656 us
  waiting for transfers between devices  352 us (54%)
  local copies, waits for them, and re-layouts  116 us (18%)
  matrix products  86.6 us (13%)
  other arithmetic  68.2 us (10%)
  between operations  14.6 us (2%)
  starting transfers between devices  13.8 us (2%)
    all_to_all x1, waiting for transfers between devices, body(): lax.all_to_all(outgoing, ('row', 'col'), split_axis=0, concat_axis=0, til...  172 us
    reduce_scatter x1, waiting for transfers between devices, body(): lax.psum_scatter(jnp.dot(left_modes.T, right_side, precision=lax.Precisio...  150 us
    slice x2, local copies, waits for them, and re-layouts, body(): mass_tile = full_pair[1]  39.5 us
    dot_general x1, matrix products, body(): jnp.dot(left_modes.T, right_side, precision=lax.Precision.HIGHEST, prefer...  30.5 us
    psum x1, waiting for transfers between devices, broadcast(): return lax.psum(kept, axis)  29.6 us
    dot_general x1, matrix products, body(): jnp.dot(stiff_tile, col_modes, preferred_element_type=jnp.float32)  24.7 us
    dot_general x1, matrix products, body(): jnp.dot(mass_off, col_modes, preferred_element_type=jnp.float32)  21.7 us
    broadcast_in_dim x1, local copies, waits for them, and re-layouts, body(): jax.ops.segment_sum(arrived, jnp.maximum(arrived_slots, 0), num_segments=...  21.2 us
  transfers between devices with their start and end apart: 5, of which 3 were waited for; matrix products, arithmetic and copies ran while one was open for 33% of the time, Pallas kernels for 0%

commit v1 on v0

--- a/solution.py
+++ b/solution.py
@@ -8,7 +8,7 @@
 
 def broadcast(value, axis, source):
     kept = jnp.where(lax.axis_index(axis) == source, value, 0).astype(value.dtype)
-    return lax.psum(kept, axis)
+    return jnp.sum(lax.all_gather(kept, axis), axis=0)
 
 
 def condense(pieces):

time: 657 us -> 692 us (1.053)
  other arithmetic: 68.2 us -> 83.5 us
  matrix products: 86.6 us -> 95.9 us
  waiting for transfers between devices: 352 us -> 360 us
    all_gather x1, waiting for transfers between devices: 0.01 us -> 118 us  [body(): col_modes = lax.all_gather(modes, 'row', axis=1, tiled=True)]
    all_to_all x1, waiting for transfers between devices: 172 us -> 91.6 us  [body(): lax.all_to_all(outgoing, ('row', 'col'), split_axis=0, concat_axis=0, til...]
    psum x1 -> x0, waiting for transfers between devices: 29.6 us -> none  [broadcast(): return lax.psum(kept, axis)]
    reduce_sum x0 -> x1, other arithmetic: none -> 12 us  [broadcast(): return jnp.sum(lax.all_gather(kept, axis), axis=0)]
    unnamed x16 -> x20, local copies, waits for them, and re-layouts: 16.4 us -> 12.3 us
  transfers between devices with their start and end apart: 5 -> 5, of which waited for: 3 -> 3; matrix products, arithmetic and copies ran while one was open for 33% -> 34% of each run, Pallas kernels for 0% -> 0%
where the time goes in v1:
time: 692 us; the launch traced here: 686 us
  waiting for transfers between devices  360 us (52%)
  local copies, waits for them, and re-layouts  114 us (16%)
  matrix products  95.9 us (14%)
  other arithmetic  83.5 us (12%)
  between operations  14.9 us (2%)
  starting transfers between devices  11.5 us (2%)
    reduce_scatter x1, waiting for transfers between devices, body(): lax.psum_scatter(jnp.dot(left_modes.T, right_side, precision=lax.Precisio...  149 us
    all_gather x1, waiting for transfers between devices, body(): col_modes = lax.all_gather(modes, 'row', axis=1, tiled=True)  118 us
    all_to_all x1, waiting for transfers between devices, body(): lax.all_to_all(outgoing, ('row', 'col'), split_axis=0, concat_axis=0, til...  91.6 us
    slice x2, local copies, waits for them, and re-layouts, body(): mass_tile = full_pair[1]  39.5 us
    dot_general x1, matrix products, body(): jnp.dot(left_modes.T, right_side, precision=lax.Precision.HIGHEST, prefer...  35.7 us
    dot_general x1, matrix products, body(): jnp.dot(stiff_tile, col_modes, preferred_element_type=jnp.float32)  27.2 us
    dot_general x1, matrix products, body(): jnp.dot(mass_off, col_modes, preferred_element_type=jnp.float32)  23.5 us
    broadcast_in_dim x1, local copies, waits for them, and re-layouts, body(): jax.ops.segment_sum(arrived, jnp.maximum(arrived_slots, 0), num_segments=...  21.4 us
  transfers between devices with their start and end apart: 5, of which 3 were waited for; matrix products, arithmetic and copies ran while one was open for 34% of the time, Pallas kernels for 0%

profile of v1, /device:TPU:0, one launch (start us, length us, event | category | flops | bytes accessed | tf_op | source)
XLA Modules:
  0.0 686.3 jit_solution(8438299642687415313)
XLA Ops:
  11.9 7.3 %all-to-all-start = ((s32[32,1,1]{2,1,0:T(1,128)}), s32[32,1,1]{2,1,0:T(1,128)S(1)}, u32[]{:S(2)}, u32[]{:S(2)}) async-start(s32[32,1,1]{2,1,0:T(1,128)} %copy.25), calls=%async_computation | async-start | bytes 32768 | tf_op jit(solution)/shard_map/all_to_all | solution.py:62
  19.4 118.4 %all-gather.4.cloned.1.call-done = bf16[4096,1024]{1,0:T(8,128)(2,1)} async-done(((bf16[4096,128]{1,0:T(8,128)(2,1)}), bf16[4096,1024]{1,0:T(8,128)(2,1)}) %all-gather.4.cloned.1.call-update) | async-done | bytes 8388624 | tf_op jit(solution)/shard_map/all_gather | solution.py:79
  137.8 5.3 dynamic-slice_select_fusion
  143.2 15.2 %while.10 = (s32[]{:T(128)}, f32[2,2,512,512]{3,2,1,0:T(8,128)}, bf16[2,512,512]{2,1,0:T(8,128)(2,1)S(1)}, bf16[2,1024,512]{2,1,0:T(8,128)(2,1)S(1)}, bf16[2,102...) while((s32[]{:T(128)}, f32[2,2,512,512]{3,2,1,0:T(8,128)}, ...), condition=%wide.region_3.4_spmd, body=%wide.region_2.3_spmd.sunk | while | flops 2151940096 | bytes 47730848 | solution.py:44
  158.4 5.3 reshape.158
  163.7 4.8 copy.26
  168.5 5.0 gather_fusion.1
  173.5 5.1 select_multiply_fusion
  184.7 91.6 %all-to-all-done.1 = f32[32,2,128,128]{3,2,1,0:T(8,128)} async-done(((f32[32,2,128,128]{3,2,1,0:T(8,128)}), f32[32,2,128,128]{3,2,1,0:T(8,128)}, u32[]{:S(2)}, u32[]{:S(2)}) %all-to-all-start.1) | async-done | bytes 4194336 | tf_op jit(solution)/shard_map/all_to_all | solution.py:61
  276.2 21.4 %broadcast_in_dim.82 = f32[512,2,128,128]{3,2,1,0:T(8,128)} broadcast(f32[]{:T(128)} %constant.134.clone.1), dimensions={} | broadcast | bytes 67108864 | tf_op jit(solution)/shard_map/broadcast_in_dim | solution.py:64
  297.6 9.7 %scatter_fusion = f32[512,2,128,128]{3,2,1,0:T(8,128)} fusion(f32[512,2,128,128]{3,2,1,0:T(8,128)} %broadcast_in_dim.82, s32[32]{0:T(128)S(1)} %maximum_reduce_fusion, f32[32,2,128,128]{3,2,1,0:T(8,128)} %all-to-all-done.1), kind=kCustom, calls=%fused_computation.2 | custom fusion | flops 1048576 | bytes 12583040 | tf_op jit(solution)/shard_map/scatter-add | solution.py:64
  307.4 27.9 %fusion.25 = (bf16[1,16,128,32,128]{4,2,0,3,1:T(8,128)(2,1)S(1)}, bf16[1,16,128,32,128]{4,2,0,3,1:T(8,128)(2,1)}) fusion(f32[2,16,128,32,128]{4,2,0,3,1:T(8,128)} %bitcast.12), kind=kLoop, calls=%fused_computation.65 | loop fusion | bytes 67108864 | tf_op jit(solution)/shard_map/slice | solution.py:74
  335.3 14.7 %copy.27 = bf16[1,16,128,32,128]{4,3,2,1,0:T(8,128)(2,1)S(1)} copy(bf16[1,16,128,32,128]{4,2,0,3,1:T(8,128)(2,1)} %get-tuple-element.62) | data formatting | bytes 33554432 | tf_op jit(solution)/shard_map/slice | solution.py:77
  350.0 11.0 %copy.35 = bf16[256,8,32,128]{3,1,2,0:T(8,128)(2,1)} copy(bf16[256,8,32,128]{3,2,1,0:T(8,128)(2,1)S(1)} %bitcast.77) | data formatting | bytes 33554432
  361.0 11.6 %copy.28 = bf16[1,16,128,32,128]{4,3,2,1,0:T(8,128)(2,1)} copy(bf16[1,16,128,32,128]{4,2,0,3,1:T(8,128)(2,1)S(1)} %get-tuple-element.61) | data formatting | bytes 33554432 | tf_op jit(solution)/shard_map/slice | solution.py:74
  372.6 14.6 %select_reduce_fusion = f32[16,128]{1,0:T(8,128)S(1)} fusion(s32[16,128]{1,0:T(8,128)S(1)} %add_add_fusion, s32[32,128]{1,0:T(8,128)S(1)} %multiply_add_fusion, pred[]{:T(512)S(6)} %eq.67, f32[2,16,128,32,128]{4,2,0,3,1:T(8,128)} %bitcast.12), kind=kLoop, calls=%fused_computation.28 | loop fusion | flops 33552384 | bytes 33587200 | tf_op jit(solution)/shard_map/reduce_sum | solution.py:75
  387.2 6.6 all-reduce
  393.8 21.1 %fusion.17 = bf16[2048,4096]{1,0:T(8,128)(2,1)} fusion(bf16[256,8,32,128]{3,2,1,0:T(8,128)(2,1)} %bitcast.76, s32[2048]{0:T(1024)S(1)} %iota_add_fusion, pred[]{:T(512)S(6)} %eq.67), kind=kLoop, calls=%fused_computation.26 | loop fusion | flops 25165824 | bytes 33562624 | tf_op jit(solution)/shard_map/convert_element_type | solution.py:78
  414.9 23.5 %fusion.28 = f32[2048,1024]{0,1:T(8,128)S(1)} fusion(bf16[2048,4096]{1,0:T(8,128)(2,1)} %fusion.17, bf16[4096,1024]{1,0:T(8,128)(2,1)} %all-gather.4.cloned.1.call-done), kind=kOutput, calls=%fused_computation.68 | convolution fusion | flops 17179869184 | bytes 33554432 | tf_op jit(solution)/shard_map/dot_general | solution.py:87
  438.4 27.2 %fusion.27 = f32[2048,1024]{0,1:T(8,128)} fusion(bf16[2048,4096]{1,0:T(8,128)(2,1)} %bitcast.79, bf16[4096,1024]{1,0:T(8,128)(2,1)} %all-gather.4.cloned.1.call-done), kind=kOutput, calls=%fused_computation.67 | convolution fusion | flops 17179869184 | bytes 33554432 | tf_op jit(solution)/shard_map/dot_general | solution.py:86
  465.6 10.0 %pad_maximum_fusion = f32[2048,2048]{0,1:T(8,128)} fusion(f32[2048,1024]{0,1:T(8,128)S(1)} %fusion.28, f32[2048,1024]{0,1:T(8,128)} %fusion.27), kind=kLoop, calls=%fused_computation.32 | loop fusion | flops 4194304 | bytes 33554432 | tf_op jit(solution)/shard_map/concatenate | solution.py:84
  475.6 12.0 %reduce_sum.23 = bf16[2048,1024]{1,0:T(8,128)(2,1)} reduce(bf16[4,2048,1024]{2,1,0:T(8,128)(2,1)} %bitcast.78, bf16[]{:T(256)} %constant.153.clone.1), dimensions={0}, to_apply=%region_5.6 | reduce | flops 6291456 | bytes 20971522 | tf_op jit(solution)/shard_map/reduce_sum | solution.py:11
  493.1 35.7 %fusion.29 = f32[1024,2048]{1,0:T(8,128)} fusion(bf16[2048,1024]{1,0:T(8,128)(2,1)S(1)} %copy-done.1, f32[2048,2048]{0,1:T(8,128)} %fusion.21), kind=kOutput, calls=%fused_computation.69 | convolution fusion | flops 51539607552 | bytes 29360128 | tf_op jit(solution)/shard_map/dot_general | solution.py:103
  528.8 149.0 %reduce-scatter.2.cloned.1.call-done = f32[32,2048]{1,0:T(8,128)} async-done(((f32[1024,2048]{1,0:T(8,128)}), f32[32,2048]{1,0:T(8,128)}) %reduce-scatter.2.cloned.1.call-update) | async-done | bytes 262160 | tf_op jit(solution)/shard_map/reduce_scatter | solution.py:102
  (69 shorter events, 32.4 us)
Async XLA Ops:
  7.2 136.0 %copy-start.8 = (bf16[2,512,512]{2,1,0:T(8,128)(2,1)S(1)}, bf16[2,512,512]{2,1,0:T(8,128)(2,1)}, u32[]{:S(2)}) copy-start(bf16[2,512,512]{2,1,0:T(8,128)(2,1)} %param.11) | copy-start | bytes 3145732
  7.2 136.0 %copy-start.7 = (bf16[2,1024,512]{2,1,0:T(8,128)(2,1)S(1)}, bf16[2,1024,512]{2,1,0:T(8,128)(2,1)}, u32[]{:S(2)}) copy-start(bf16[2,1024,512]{2,1,0:T(8,128)(2,1)} %param.10) | copy-start | bytes 6291460
  7.2 136.0 %copy-start.4 = (f32[2,1024]{1,0:T(2,128)S(1)}, f32[2,1024]{1,0:T(2,128)}, u32[]{:S(2)}) copy-start(f32[2,1024]{1,0:T(2,128)} %param.12) | copy-start | bytes 24580
  7.2 136.0 %copy-start.5 = (f32[2,512]{1,0:T(2,128)S(1)}, f32[2,512]{1,0:T(2,128)}, u32[]{:S(2)}) copy-start(f32[2,512]{1,0:T(2,128)} %param.13) | copy-start | bytes 12292
  7.2 130.5 %all-gather.4.cloned.1.call-start = ((), (), s32[]{:S(2)}) async-start(), calls=%async_computation.3 | async-start | bytes 9437184 | tf_op jit(solution)/shard_map/all_gather | solution.py:79
  11.9 166.7 %all-to-all-start = ((s32[32,1,1]{2,1,0:T(1,128)}), s32[32,1,1]{2,1,0:T(1,128)S(1)}, u32[]{:S(2)}, u32[]{:S(2)}) async-start(s32[32,1,1]{2,1,0:T(1,128)} %copy.25), calls=%async_computation | async-start | bytes 32768 | tf_op jit(solution)/shard_map/all_to_all | solution.py:62
  19.3 456.3 %all-gather.6.cloned.1.call-start = ((), (), s32[]{:S(2)}) async-start(), calls=%async_computation.5 | async-start | bytes 20971520 | tf_op jit(solution)/shard_map/all_gather | solution.py:11
  143.2 4.7 copy-start.2
  148.1 2.2 copy-start.3
  150.3 5.0 copy-start.2
  155.6 2.8 copy-start.3
  173.5 9.2 %copy-start.9 = (u32[32]{0:T(128)S(1)}, u32[32]{0:T(128)}, u32[]{:S(2)}) copy-start(u32[32]{0:T(128)} %constant.165) | copy-start | bytes 388
  178.6 97.6 %all-to-all-start.1 = ((f32[32,2,128,128]{3,2,1,0:T(8,128)}), f32[32,2,128,128]{3,2,1,0:T(8,128)}, u32[]{:S(2)}, u32[]{:S(2)}) async-start(f32[32,2,128,128]{3,2,1,0:T(8,128)} %select_multiply_fusion), calls=%async_computation.1 | async-start | bytes 8388608 | tf_op jit(solution)/shard_map/all_to_all | solution.py:61
  182.2 495.6 %reduce-scatter.2.cloned.1.call-start = ((), (), s32[]{:S(2)}) async-start(), calls=%async_computation.4 | async-start | bytes 8650752 | tf_op jit(solution)/shard_map/reduce_scatter | solution.py:102
  393.8 95.7 %copy-start.6 = (f32[512]{0:T(512)}, f32[512]{0:T(512)S(1)}, u32[]{:S(2)}) copy-start(f32[512]{0:T(512)S(1)} %dynamic-slice.1) | copy-start | bytes 6148
  438.4 27.2 %copy-start = (f32[2048,1024]{0,1:T(8,128)}, f32[2048,1024]{0,1:T(8,128)S(1)}, u32[]{:S(2)}) copy-start(f32[2048,1024]{0,1:T(8,128)S(1)} %fusion.28) | copy-start | bytes 25165828
  489.5 3.5 copy-start.1
Sparse Core Ops, SparseCore 0:
  10.1 127.6 all-gather.3
  143.2 149.0 all-gather.5
  528.9 148.8 reduce-scatter.1
